TPU v7x, 32 devices: a whole 2x2x4 slice. The times are simulated.
32 devices in a mesh: dp: 8 (over y, x, core), seq: 4 (over z).
Axes of the slice: x: 2, y: 2, z: 4, core: 2. Of those that a mesh axis runs over, the one named last changes fastest.
Arguments:
- tokens: bfloat16 [96, 200, 512], P('dp', 'seq'), may hold values from -6 to 6
- ln1_gain: bfloat16 [512], P('dp'), may hold values from 0.5 to 1.5
- ln1_bias: bfloat16 [512], P('dp'), may hold values from -1 to 1
- w_qkv: bfloat16 [512, 1536], P('dp'), may hold values from -0.25 to 0.25
- w_out: bfloat16 [512, 512], P('dp'), may hold values from -1.75 to 1.75
- ln2_gain: bfloat16 [512], P('dp'), may hold values from 0.5 to 1.5
- ln2_bias: bfloat16 [512], P('dp'), may hold values from -1 to 1
- w_router: bfloat16 [512, 8], P('dp'), may hold values from -0.1875 to 0.1875
- expert_in: bfloat16 [8, 512, 2048], P('dp', None, 'seq'), may hold values from -0.25 to 0.25
- expert_out: bfloat16 [8, 2048, 512], P('dp', 'seq'), may hold values from -3 to 3
- routes: int32 [96, 200, 2], P('dp', 'seq'), may hold values from 0 to 7, all different within a row; in each aligned block of 50 rows (0 to 49, 50 to 99, ..., all dimensions but the last counted through in order) at most 14 rows name the same one
- targets: bfloat16 [96, 200, 512], P('dp', 'seq'), may hold values from -6 to 6
Outputs:
- mixed: bfloat16 [96, 200, 512], P('dp', 'seq')
- grad_tokens: float32 [96, 200, 512], P('dp', 'seq')
- grad_ln1_gain: float32 [512], P('dp')
- grad_ln1_bias: float32 [512], P('dp')
- grad_qkv: float32 [512, 1536], P('dp')
- grad_out: float32 [512, 512], P('dp')
- grad_ln2_gain: float32 [512], P('dp')
- grad_ln2_bias: float32 [512], P('dp')
- grad_router: float32 [512, 8], P('dp')
- grad_expert_in: float32 [8, 512, 2048], P('dp', None, 'seq')
- grad_expert_out: float32 [8, 2048, 512], P('dp', 'seq')
Inputs may be any that keep to these rules, and one draw needn't show every extreme that they name: `routes`: each slot names two different experts. In each aligned block of 50 rows (one image's slots on one device), no expert is named more than 14 times, and some expert reaches 14.
All inputs are finite; a program needn't handle non-finite values.
Results may differ from a plain program's by a relative error of at most 0.013.
Values may be sent and summed in bfloat16 or wider, within the bound.
A program may use at most 128 MiB of HBM per device.

v0:
```python
import jax
import jax.numpy as jnp
from jax import lax
from jax.sharding import PartitionSpec as P

H = 8
S = 200
VALID = 197


def layer_norm(values, gain_vec, bias_vec):
    centre = values - jnp.mean(values, axis=-1, keepdims=True)
    spread = jnp.mean(centre * centre, axis=-1, keepdims=True)
    return centre * lax.rsqrt(spread + 1e-06) * gain_vec + bias_vec


def regroup_heads(values):
    return lax.all_to_all(values, "seq", split_axis=3, concat_axis=1, tiled=True)


def regroup_slots(values):
    return lax.all_to_all(values, "seq", split_axis=1, concat_axis=3, tiled=True)


def send_experts(values):
    return lax.all_to_all(values, "dp", split_axis=0, concat_axis=1, tiled=True)


def send_tokens(values):
    return lax.all_to_all(values, "dp", split_axis=1, concat_axis=0, tiled=True)


def masked_scores(queries, keys_in, key_valid):
    scores = (
        jnp.einsum("bqhd,bkhd->bhqk", queries, keys_in, preferred_element_type=jnp.float32) * 0.125
    )
    return jnp.where(key_valid, scores, -1e30)


def attention_forward(queries, keys_in, values, key_valid):
    scores = masked_scores(queries, keys_in, key_valid)
    row_top = jnp.max(scores, axis=-1, keepdims=True)
    exponent = jnp.exp(scores - row_top)
    row_total = jnp.sum(exponent, axis=-1, keepdims=True)
    prob_rows = exponent / row_total
    log_total = row_top + jnp.log(row_total)
    attended = jnp.einsum(
        "bhqk,bkhd->bqhd",
        prob_rows.astype(jnp.bfloat16),
        values,
        preferred_element_type=jnp.float32,
    )
    return (attended.astype(jnp.bfloat16), log_total)


def attention_backward(queries, keys_in, values, log_total, grad_attended, key_valid):
    scores = masked_scores(queries, keys_in, key_valid)
    prob_rows = jnp.exp(scores - log_total)
    grad_values = jnp.einsum(
        "bhqk,bqhd->bkhd",
        prob_rows.astype(jnp.bfloat16),
        grad_attended,
        preferred_element_type=jnp.float32,
    )
    grad_probs = jnp.einsum(
        "bqhd,bkhd->bhqk", grad_attended, values, preferred_element_type=jnp.float32
    )
    inner_sum = jnp.sum(prob_rows * grad_probs, axis=-1, keepdims=True)
    grad_scores = (prob_rows * (grad_probs - inner_sum)).astype(jnp.bfloat16)
    grad_queries = (
        jnp.einsum("bhqk,bkhd->bqhd", grad_scores, keys_in, preferred_element_type=jnp.float32)
        * 0.125
    )
    grad_keys = (
        jnp.einsum("bhqk,bqhd->bkhd", grad_scores, queries, preferred_element_type=jnp.float32)
        * 0.125
    )
    return jnp.stack([grad_queries, grad_keys, grad_values], axis=2)


def pick_block(total_rows):
    for candidate in (1024, 768, 512, 384, 256):
        if total_rows % candidate == 0:
            return candidate
    return total_rows


def local(
    tokens,
    ln1_gain,
    ln1_bias,
    w_qkv,
    w_out,
    ln2_gain,
    ln2_bias,
    w_router,
    expert_in,
    expert_out,
    routes,
    targets,
):
    image_count, slot_count, model_width = tokens.shape
    seq_devices = lax.axis_size("seq")
    row_count = image_count * slot_count
    expert_count = w_router.shape[1]
    local_experts = expert_in.shape[0]
    slot_limit = 2 * S // (seq_devices * expert_count) + 2
    head_size = model_width // H
    gathered = (
        lax.all_gather(ln1_gain, "dp", axis=0, tiled=True),
        lax.all_gather(ln1_bias, "dp", axis=0, tiled=True),
        lax.all_gather(w_qkv, "dp", axis=0, tiled=True),
        lax.all_gather(w_out, "dp", axis=0, tiled=True),
        lax.all_gather(ln2_gain, "dp", axis=0, tiled=True),
        lax.all_gather(ln2_bias, "dp", axis=0, tiled=True),
        lax.all_gather(w_router, "dp", axis=0, tiled=True),
    )
    gain_one = gathered[0].astype(jnp.float32)
    bias_one = gathered[1].astype(jnp.float32)
    qkv_weight = gathered[2]
    out_weight = gathered[3]
    gain_two = gathered[4].astype(jnp.float32)
    bias_two = gathered[5].astype(jnp.float32)
    router_weight = gathered[6]
    slot_start = lax.axis_index("seq") * slot_count
    valid_slot = slot_start + jnp.arange(slot_count) < VALID
    valid_rows = jnp.tile(valid_slot, image_count)
    key_valid = (jnp.arange(S) < VALID)[None, None, None, :]
    token_rows = tokens.reshape(row_count, model_width).astype(jnp.float32)
    normed_one, norm_one_back = jax.vjp(layer_norm, token_rows, gain_one, bias_one)
    normed_one_b = normed_one.astype(jnp.bfloat16)
    mixed_qkv = jnp.dot(normed_one_b, qkv_weight, preferred_element_type=jnp.float32).astype(
        jnp.bfloat16
    )
    qkv_heads = regroup_heads(mixed_qkv.reshape(image_count, slot_count, 3, H, head_size))
    queries = qkv_heads[:, :, 0]
    keys_in = qkv_heads[:, :, 1]
    values = qkv_heads[:, :, 2]
    attended, log_total = attention_forward(queries, keys_in, values, key_valid)
    attended_rows = regroup_slots(attended[:, :, None]).reshape(row_count, model_width)
    residual_two = token_rows + jnp.dot(
        attended_rows, out_weight, preferred_element_type=jnp.float32
    )
    normed_two, norm_two_back = jax.vjp(layer_norm, residual_two, gain_two, bias_two)
    normed_two_b = normed_two.astype(jnp.bfloat16)
    logits = jnp.dot(normed_two_b, router_weight, preferred_element_type=jnp.float32)
    route_rows = routes.reshape(row_count, 2)
    chosen = (route_rows[:, :, None] == jnp.arange(expert_count)[None, None, :]) & valid_rows[
        :, None, None
    ]
    chosen_f = chosen.astype(jnp.float32)

    def gate_pick(logit_rows):
        return jnp.sum(jax.nn.softmax(logit_rows, axis=-1)[:, None, :] * chosen_f, axis=-1)

    gate_values, gate_back = jax.vjp(gate_pick, logits)
    pick_count = chosen.astype(jnp.int32).reshape(image_count, slot_count * 2, expert_count)
    before = jnp.cumsum(pick_count, axis=1) - pick_count
    place_hit = (before[..., None] == jnp.arange(slot_limit)) & (pick_count[..., None] > 0)
    dispatch = place_hit.astype(jnp.bfloat16).reshape(
        image_count, slot_count, 2, expert_count, slot_limit
    )
    normed_img = normed_two_b.reshape(image_count, slot_count, model_width)
    sent_rows = jnp.einsum(
        "bskem,bsd->ebmd", dispatch, normed_img, preferred_element_type=jnp.float32
    ).astype(jnp.bfloat16)
    received = send_experts(sent_rows.reshape(expert_count, image_count * slot_limit, model_width))
    weights_in, weights_out = (
        lax.all_gather(expert_in, "seq", axis=2, tiled=True),
        lax.all_gather(expert_out, "seq", axis=1, tiled=True),
    )
    total_rows = received.shape[1]
    block_rows = pick_block(total_rows)
    block_count = total_rows // block_rows

    def expert_step(block_index, produced):
        row_piece = lax.dynamic_slice_in_dim(received, block_index * block_rows, block_rows, 1)
        hidden_pre = jnp.einsum(
            "erd,edf->erf", row_piece, weights_in, preferred_element_type=jnp.float32
        )
        activated = jax.nn.gelu(hidden_pre).astype(jnp.bfloat16)
        result = jnp.einsum(
            "erf,efd->erd", activated, weights_out, preferred_element_type=jnp.float32
        ).astype(jnp.bfloat16)
        return lax.dynamic_update_slice_in_dim(produced, result, block_index * block_rows, 1)

    produced = lax.fori_loop(
        0,
        block_count,
        expert_step,
        jnp.zeros((local_experts, total_rows, model_width), jnp.bfloat16),
    )
    returned = send_tokens(produced).reshape(expert_count, image_count, slot_limit, model_width)
    per_choice = jnp.einsum(
        "bskem,ebmd->bskd", dispatch, returned, preferred_element_type=jnp.float32
    ).reshape(row_count, 2, model_width)
    mixed_rows = (
        residual_two
        + gate_values[:, 0:1] * per_choice[:, 0]
        + gate_values[:, 1:2] * per_choice[:, 1]
    )
    target_rows = targets.reshape(row_count, model_width).astype(jnp.float32)
    grad_mixed = (mixed_rows - target_rows) * valid_rows[:, None].astype(jnp.float32)
    grad_gates = jnp.sum(grad_mixed[:, None, :] * per_choice, axis=-1)
    grad_choice = (
        (gate_values[:, :, None] * grad_mixed[:, None, :])
        .astype(jnp.bfloat16)
        .reshape(image_count, slot_count, 2, model_width)
    )
    grad_sent = jnp.einsum(
        "bskem,bskd->ebmd", dispatch, grad_choice, preferred_element_type=jnp.float32
    ).astype(jnp.bfloat16)
    grad_received = send_experts(
        grad_sent.reshape(expert_count, image_count * slot_limit, model_width)
    )
    back_in, back_out = (
        lax.all_gather(expert_in, "seq", axis=2, tiled=True),
        lax.all_gather(expert_out, "seq", axis=1, tiled=True),
    )

    def expert_back(block_index, loop_carry):
        grad_in_sum, grad_out_sum, grad_rows = loop_carry
        row_piece = lax.dynamic_slice_in_dim(received, block_index * block_rows, block_rows, 1)
        grad_piece = lax.dynamic_slice_in_dim(
            grad_received, block_index * block_rows, block_rows, 1
        )
        hidden_pre = jnp.einsum(
            "erd,edf->erf", row_piece, back_in, preferred_element_type=jnp.float32
        )
        activated, gelu_back = jax.vjp(jax.nn.gelu, hidden_pre)
        grad_act = jnp.einsum(
            "erd,efd->erf", grad_piece, back_out, preferred_element_type=jnp.float32
        )
        grad_pre = gelu_back(grad_act)[0].astype(jnp.bfloat16)
        grad_out_sum = grad_out_sum + jnp.einsum(
            "erf,erd->efd",
            activated.astype(jnp.bfloat16),
            grad_piece,
            preferred_element_type=jnp.float32,
        )
        grad_in_sum = grad_in_sum + jnp.einsum(
            "erd,erf->edf", row_piece, grad_pre, preferred_element_type=jnp.float32
        )
        rows_back = jnp.einsum(
            "erf,edf->erd", grad_pre, back_in, preferred_element_type=jnp.float32
        ).astype(jnp.bfloat16)
        grad_rows = lax.dynamic_update_slice_in_dim(
            grad_rows, rows_back, block_index * block_rows, 1
        )
        return (grad_in_sum, grad_out_sum, grad_rows)

    start_carry = (
        jnp.zeros(back_in.shape, jnp.float32),
        jnp.zeros(back_out.shape, jnp.float32),
        jnp.zeros((local_experts, total_rows, model_width), jnp.bfloat16),
    )
    grad_in_sum, grad_out_sum, grad_rows = lax.fori_loop(0, block_count, expert_back, start_carry)
    grad_returned = send_tokens(grad_rows).reshape(
        expert_count, image_count, slot_limit, model_width
    )
    grad_normed_two = jnp.einsum(
        "bskem,ebmd->bsd", dispatch, grad_returned, preferred_element_type=jnp.float32
    ).reshape(row_count, model_width)
    grad_logits = gate_back(grad_gates)[0].astype(jnp.bfloat16)
    grad_router = jnp.einsum(
        "rd,re->de", normed_two_b, grad_logits, preferred_element_type=jnp.float32
    )
    grad_normed_two = grad_normed_two + jnp.einsum(
        "re,de->rd", grad_logits, router_weight, preferred_element_type=jnp.float32
    )
    grad_res_two, grad_gain_two, grad_bias_two = norm_two_back(grad_normed_two)
    grad_residual = grad_mixed + grad_res_two
    grad_branch = grad_residual.astype(jnp.bfloat16)
    grad_out_weight = jnp.einsum(
        "rd,re->de", attended_rows, grad_branch, preferred_element_type=jnp.float32
    )
    grad_attended = jnp.einsum(
        "re,de->rd", grad_branch, out_weight, preferred_element_type=jnp.float32
    ).astype(jnp.bfloat16)
    grad_heads = regroup_heads(grad_attended.reshape(image_count, slot_count, 1, H, head_size))[
        :, :, 0
    ]
    grad_qkv_heads = attention_backward(
        queries, keys_in, values, log_total, grad_heads, key_valid
    ).astype(jnp.bfloat16)
    grad_qkv_rows = regroup_slots(grad_qkv_heads).reshape(row_count, 3 * model_width)
    grad_qkv_weight = jnp.einsum(
        "rd,rf->df", normed_one_b, grad_qkv_rows, preferred_element_type=jnp.float32
    )
    grad_normed_one = jnp.einsum(
        "rf,df->rd", grad_qkv_rows, qkv_weight, preferred_element_type=jnp.float32
    )
    grad_token_ln, grad_gain_one, grad_bias_one = norm_one_back(grad_normed_one)
    grad_tokens = grad_residual + grad_token_ln
    dense_grads = (
        grad_gain_one,
        grad_bias_one,
        grad_qkv_weight,
        grad_out_weight,
        grad_gain_two,
        grad_bias_two,
        grad_router,
    )
    dense_grads = (
        lax.psum(dense_grads[0].astype(jnp.bfloat16), "seq").astype(jnp.float32),
        lax.psum(dense_grads[1].astype(jnp.bfloat16), "seq").astype(jnp.float32),
        lax.psum(dense_grads[2].astype(jnp.bfloat16), "seq").astype(jnp.float32),
        lax.psum(dense_grads[3].astype(jnp.bfloat16), "seq").astype(jnp.float32),
        lax.psum(dense_grads[4].astype(jnp.bfloat16), "seq").astype(jnp.float32),
        lax.psum(dense_grads[5].astype(jnp.bfloat16), "seq").astype(jnp.float32),
        lax.psum(dense_grads[6].astype(jnp.bfloat16), "seq").astype(jnp.float32),
    )
    dense_grads = (
        lax.psum_scatter(
            dense_grads[0].astype(jnp.bfloat16), "dp", scatter_dimension=0, tiled=True
        ).astype(jnp.float32),
        lax.psum_scatter(
            dense_grads[1].astype(jnp.bfloat16), "dp", scatter_dimension=0, tiled=True
        ).astype(jnp.float32),
        lax.psum_scatter(
            dense_grads[2].astype(jnp.bfloat16), "dp", scatter_dimension=0, tiled=True
        ).astype(jnp.float32),
        lax.psum_scatter(
            dense_grads[3].astype(jnp.bfloat16), "dp", scatter_dimension=0, tiled=True
        ).astype(jnp.float32),
        lax.psum_scatter(
            dense_grads[4].astype(jnp.bfloat16), "dp", scatter_dimension=0, tiled=True
        ).astype(jnp.float32),
        lax.psum_scatter(
            dense_grads[5].astype(jnp.bfloat16), "dp", scatter_dimension=0, tiled=True
        ).astype(jnp.float32),
        lax.psum_scatter(
            dense_grads[6].astype(jnp.bfloat16), "dp", scatter_dimension=0, tiled=True
        ).astype(jnp.float32),
    )
    expert_in_grad, expert_out_grad = (
        lax.psum_scatter(
            grad_in_sum.astype(jnp.bfloat16), "seq", scatter_dimension=2, tiled=True
        ).astype(jnp.float32),
        lax.psum_scatter(
            grad_out_sum.astype(jnp.bfloat16), "seq", scatter_dimension=1, tiled=True
        ).astype(jnp.float32),
    )
    mixed = mixed_rows.astype(jnp.bfloat16).reshape(image_count, slot_count, model_width)
    return (
        mixed,
        grad_tokens.reshape(image_count, slot_count, model_width),
        dense_grads[0],
        dense_grads[1],
        dense_grads[2],
        dense_grads[3],
        dense_grads[4],
        dense_grads[5],
        dense_grads[6],
        expert_in_grad,
        expert_out_grad,
    )


def solution(mesh):
    placed = (
        P("dp", "seq", None),
        P("dp"),
        P("dp"),
        P("dp", None),
        P("dp", None),
        P("dp"),
        P("dp"),
        P("dp", None),
        P("dp", None, "seq"),
        P("dp", "seq", None),
        P("dp", "seq", None),
        P("dp", "seq", None),
    )
    return jax.shard_map(
        local,
        mesh=mesh,
        in_specs=placed,
        out_specs=(
            P("dp", "seq", None),
            P("dp", "seq", None),
            P("dp"),
            P("dp"),
            P("dp", None),
            P("dp", None),
            P("dp"),
            P("dp"),
            P("dp", None),
            P("dp", None, "seq"),
            P("dp", "seq", None),
        ),
        check_vma=False,
    )
```

profile of v0, /device:TPU:0, one launch (start us, length us, event | category | flops | bytes accessed | tf_op | source)
XLA Modules:
  0.0 738.3 jit_solution(14534104639926114627)
XLA Ops:
  12.9 15.1 %all-reduce.9 = (bf16[512]{0:T(512)(128)(2,1)S(1)}, bf16[512]{0:T(512)(128)(2,1)S(1)}, bf16[512]{0:T(512)(128)(2,1)S(1)}, bf16[512]{0:T(512)(128)(2,1)S(1)}) all-reduce(bf16[512]{0:T(512)(128)(2,1)S(1)} %dynamic-update-slice.1, bf16[512]{0:T(512)(128)(2,1)S(1)} %dynamic-update-slice, ...), channel_id=1, replica_groups=mesh['dp'=8,'seq'=4] {'dp'}, use_global_device_ids=true, to_apply=%add.1 | all-reduce | flops 2048 | bytes 8192
  28.8 9.6 %all-gather.5.cloned.1.call-done = bf16[512,1536]{1,0:T(8,128)(2,1)} async-done(((bf16[64,1536]{1,0:T(8,128)(2,1)}), bf16[512,1536]{1,0:T(8,128)(2,1)}) %all-gather.5.cloned.1.call-update) | async-done | bytes 1572880 | tf_op jit(solution)/shard_map/all_gather | solution.py:112
  64.0 81.6 %all-to-all-done = bf16[4,2,115200]{2,1,0:T(2,128)(2,1)} async-done(((bf16[4,2,115200]{2,1,0:T(2,128)(2,1)}), bf16[4,2,115200]{2,1,0:T(2,128)(2,1)}, u32[]{:S(2)}, u32[]{:S(2)}) %all-to-all-start) | async-done | bytes 1843232 | tf_op jit(solution)/shard_map/all_to_all | solution.py:18
  157.1 12.8 %copy.287 = bf16[12,4,50,3,2,64]{2,1,5,4,0,3:T(4,128)(2,1)} copy(bf16[12,4,50,3,2,64]{5,4,1,3,2,0:T(2,128)(2,1)} %bitcast.197) | data formatting | bytes 3686400 | tf_op jit(solution)/shard_map/all_to_all | solution.py:18
  201.3 22.7 %all_gather.32 = bf16[512,512]{1,0:T(8,128)(2,1)} all-gather(bf16[64,512]{1,0:T(8,128)(2,1)S(1)} %copy-done.18), channel_id=1, replica_groups=mesh['dp'=8,'seq'=4] {'dp'}, dimensions={0}, use_global_device_ids=true | all-gather | bytes 589824 | tf_op jit(solution)/shard_map/all_gather | solution.py:113
  245.4 18.9 %all-to-all-done.2 = bf16[8,168,512]{2,1,0:T(8,128)(2,1)} async-done(((bf16[8,168,512]{2,1,0:T(8,128)(2,1)}), bf16[8,168,512]{2,1,0:T(8,128)(2,1)}, u32[]{:S(2)}, u32[]{:S(2)}) %all-to-all-start.2) | async-done | bytes 1376288 | tf_op jit(solution)/shard_map/all_to_all | solution.py:26
  264.3 9.8 %multiply_convert_fusion = (bf16[1344,2048]{1,0:T(8,128)(2,1)}, f32[1344,2048]{1,0:T(8,128)}) fusion(bf16[1344,512]{1,0:T(8,128)(2,1)} %bitcast.15, bf16[1,512,2048]{2,1,0:T(8,128)(2,1)} %all-gather.7.cloned.1.call-done), kind=kOutput, calls=%fused_computation.9 | convolution fusion | flops 2843344896 | bytes 19988480 | tf_op jit(solution)/shard_map/while/body/eval_jaxpr/erd,edf->erf/dot_general | solution.py:178
  280.3 12.5 %copy.321 = bf16[1,1344,512]{2,0,1:T(2,128)(2,1)} copy(bf16[1,1344,512]{2,1,0:T(8,128)(2,1)S(1)} %fusion.15) | data formatting | bytes 2752512 | tf_op jit(solution)/shard_map/while/body/eval_jaxpr/convert_element_type | solution.py:184
  293.3 10.9 %reduce.11 = bf16[1344,512]{1,0:T(8,128)(2,1)} reduce(bf16[1344,1,512]{2,1,0:T(2,128)(2,1)} %bitcast.200, bf16[]{:T(256)} %broadcast.305), dimensions={1}, to_apply=%bitcast.187.reduce_sub_computation | reduce | bytes 2752514
  313.9 21.3 %all-gather = bf16[8,64,8]{1,2,0:T(8,128)(2,1)S(1)} all-gather(bf16[1,64,8]{1,2,0:T(8,128)(2,1)S(1)} %bitcast.217), channel_id=1, replica_groups=mesh['dp'=8,'seq'=4] {'dp'}, dimensions={0}, use_global_device_ids=true | all-gather | bytes 9216 | tf_op jit(solution)/shard_map/all_gather | solution.py:116
  352.1 10.3 %bitcast_reduce_fusion.1 = bf16[1344,512]{1,0:T(8,128)(2,1)} fusion(bf16[1344,1,512]{2,1,0:T(2,128)(2,1)} %reshape.423), kind=kLoop, calls=%fused_computation.149 | loop fusion | bytes 2752512 | tf_op jit(solution)/shard_map/all_to_all | solution.py:30
  390.5 13.2 %all-to-all-done.4 = bf16[8,168,512]{2,1,0:T(8,128)(2,1)} async-done(((bf16[8,168,512]{2,1,0:T(8,128)(2,1)}), bf16[8,168,512]{2,1,0:T(8,128)(2,1)}, u32[]{:S(2)}, u32[]{:S(2)}) %all-to-all-start.4) | async-done | bytes 1376288 | tf_op jit(solution)/shard_map/all_to_all | solution.py:26
  403.7 12.5 %fusion.6 = bf16[1344,2048]{1,0:T(8,128)(2,1)S(1)} fusion(f32[1344,2048]{1,0:T(8,128)} %get-tuple-element.96, bf16[1344,512]{1,0:T(8,128)(2,1)} %bitcast.31, bf16[1,2048,512]{2,1,0:T(8,128)(2,1)} %all-gather.9.cloned.1.call-done), kind=kOutput, calls=%fused_computation.8 | convolution fusion | flops 2873622528 | bytes 19988480 | tf_op jit(solution)/shard_map/while/body/eval_jaxpr/erd,efd->erf/dot_general | solution.py:231
  419.4 12.5 %copy.320 = bf16[1,1344,512]{2,0,1:T(2,128)(2,1)} copy(bf16[1,1344,512]{2,1,0:T(8,128)(2,1)S(1)} %fusion.16) | data formatting | bytes 2752512 | tf_op jit(solution)/shard_map/while/body/eval_jaxpr/convert_element_type | solution.py:246
  431.8 10.9 %reduce.12 = bf16[1344,512]{1,0:T(8,128)(2,1)} reduce(bf16[1344,1,512]{2,1,0:T(2,128)(2,1)} %bitcast.201, bf16[]{:T(256)} %broadcast.305), dimensions={1}, to_apply=%bitcast.186.reduce_sub_computation | reduce | bytes 2752514
  459.7 11.1 %all-to-all-done.5 = bf16[8,2,43008]{2,1,0:T(2,128)(2,1)} async-done(((bf16[8,2,43008]{2,1,0:T(2,128)(2,1)}), bf16[8,2,43008]{2,1,0:T(2,128)(2,1)}, u32[]{:S(2)}, u32[]{:S(2)}) %all-to-all-start.5) | async-done | bytes 1376288 | tf_op jit(solution)/shard_map/all_to_all | solution.py:30
  476.9 10.3 %bitcast_reduce_fusion = bf16[1344,512]{1,0:T(8,128)(2,1)} fusion(bf16[1344,1,512]{2,1,0:T(2,128)(2,1)} %reshape.425), kind=kLoop, calls=%fused_computation.148 | loop fusion | bytes 2752512 | tf_op jit(solution)/shard_map/all_to_all | solution.py:30
  549.4 8.8 %copy.268 = bf16[12,200,3,2,64]{4,3,0,2,1:T(2,128)(2,1)} copy(bf16[12,200,3,2,64]{1,4,3,0,2:T(8,128)(2,1)} %pad_maximum_fusion) | data formatting | bytes 3686400 | tf_op jit(solution)/shard_map/stack | solution.py:78
  573.1 34.0 %all-to-all-done.7 = bf16[4,2,115200]{2,1,0:T(2,128)(2,1)} async-done(((bf16[4,2,115200]{2,1,0:T(2,128)(2,1)}), bf16[4,2,115200]{2,1,0:T(2,128)(2,1)}, u32[]{:S(2)}, u32[]{:S(2)}) %all-to-all-start.7) | async-done | bytes 1843232 | tf_op jit(solution)/shard_map/all_to_all | solution.py:22
  612.4 13.1 %copy.284 = bf16[12,4,50,3,2,64]{2,1,5,4,3,0:T(4,128)(2,1)} copy(bf16[12,4,50,3,2,64]{5,4,0,3,2,1:T(2,128)(2,1)} %bitcast.199) | data formatting | bytes 3686400 | tf_op jit(solution)/shard_map/all_to_all | solution.py:22
  625.5 13.2 %copy.270 = bf16[12,50,3,4,2,64]{5,4,3,2,1,0:T(2,128)(2,1)} copy(bf16[12,50,3,4,2,64]{1,3,5,4,2,0:T(4,128)(2,1)} %bitcast.194) | data formatting | bytes 3686400 | tf_op jit(solution)/shard_map/all_to_all | solution.py:22
  660.1 16.9 %all-reduce.8 = (bf16[512]{0:T(512)(128)(2,1)S(1)}, bf16[512]{0:T(512)(128)(2,1)S(1)}, bf16[512]{0:T(512)(128)(2,1)S(1)}, bf16[512]{0:T(512)(128)(2,1)S(1)}) all-reduce(bf16[512]{0:T(512)(128)(2,1)S(1)} %get-tuple-element.49, bf16[512]{0:T(512)(128)(2,1)S(1)} %get-tuple-element.61, ...), channel_id=2, replica_groups=mesh['dp'=8,'seq'=4] {'dp'}, use_global_device_ids=true, to_apply=%region_21.22.clone | all-reduce | flops 2048 | bytes 8192
  677.3 8.5 %all-reduce.10 = (bf16[64]{0:T(256)(128)(2,1)S(1)}, bf16[64]{0:T(256)(128)(2,1)S(1)}, bf16[64]{0:T(256)(128)(2,1)S(1)}, bf16[64]{0:T(256)(128)(2,1)S(1)}, bf16[64,8]{0,1:T(8,128)(2,1)S(1)}) all-reduce(bf16[64]{0:T(256)(128)(2,1)S(1)} %dynamic-slice.5, bf16[64]{0:T(256)(128)(2,1)S(1)} %dynamic-slice.7, ...), channel_id=1, replica_groups=mesh['dp'=8,'seq'=4] {'seq'}, use_global_device_ids=true, to_apply=%region_20.21 | all-reduce | flops 768 | bytes 3072 | tf_op jit(solution)/shard_map/psum | solution.py:305
  693.9 34.4 %all-reduce.14.cloned.1.call-done = (bf16[64,1536]{1,0:T(8,128)(2,1)}, bf16[64,512]{1,0:T(8,128)(2,1)}) async-done(((bf16[64,1536]{1,0:T(8,128)(2,1)}, bf16[64,512]{1,0:T(8,128)(2,1)}), (bf16[64,1536]{1,0:T(8,128)(2,1)}, bf16[64,512]{1,0:T(8,128)(2,1)})) %all-reduce.14.cloned.1.call-update) | async-done | bytes 262160 | tf_op jit(solution)/shard_map/psum | solution.py:307
  (298 shorter events, 296.9 us)
Async XLA Ops:
  7.2 31.2 %all-gather.5.cloned.1.call-start = ((), (), s32[]{:S(2)}) async-start(), calls=%async_computation.13 | async-start | bytes 1769472 | tf_op jit(solution)/shard_map/all_gather | solution.py:112
  7.9 237.5 %all-gather.7.cloned.1.call-start = ((), (), s32[]{:S(2)}) async-start(), calls=%async_computation.14 | async-start | bytes 2621440 | tf_op jit(solution)/shard_map/all_gather | solution.py:169
  10.0 32.2 %copy-start.12 = (f32[12,50]{1,0:T(8,128)}, f32[12,50]{1,0:T(8,128)S(1)}, u32[]{:S(2)}) copy-start(f32[12,50]{1,0:T(8,128)S(1)} %broadcast_multiply_fusion) | copy-start | bytes 7204
  10.5 31.8 %copy-start.31 = (f32[600]{0:T(1024)}, f32[600]{0:T(1024)S(1)}, u32[]{:S(2)}) copy-start(f32[600]{0:T(1024)S(1)} %div.69) | copy-start | bytes 7204
  58.1 87.5 %all-to-all-start = ((bf16[4,2,115200]{2,1,0:T(2,128)(2,1)}), bf16[4,2,115200]{2,1,0:T(2,128)(2,1)}, u32[]{:S(2)}, u32[]{:S(2)}) async-start(bf16[4,2,115200]{2,1,0:T(2,128)(2,1)} %reshape.418), calls=%async_computation | async-start | bytes 3686400 | tf_op jit(solution)/shard_map/all_to_all | solution.py:18
  62.8 211.3 %all-gather.9.cloned.1.call-start = ((), (), s32[]{:S(2)}) async-start(), calls=%async_computation.15 | async-start | bytes 2621440 | tf_op jit(solution)/shard_map/all_gather | solution.py:170
  63.6 137.7 %copy-start.41 = (pred[50]{0:T(512)(128)(4,1)}, pred[50]{0:T(512)(128)(4,1)S(1)}, u32[]{:S(2)}) copy-start(pred[50]{0:T(512)(128)(4,1)S(1)} %add_compare_fusion) | copy-start | bytes 154
  187.0 37.6 %all-to-all-start.1 = ((bf16[4,2,38400]{2,1,0:T(2,128)(2,1)}), bf16[4,2,38400]{2,1,0:T(2,128)(2,1)S(1)}, u32[]{:S(2)}, u32[]{:S(2)}) async-start(bf16[4,2,38400]{2,1,0:T(2,128)(2,1)} %reshape.420), calls=%async_computation.1 | async-start | bytes 1228800 | tf_op jit(solution)/shard_map/all_to_all | solution.py:22
  194.3 41.5 %copy-start.26 = (f32[512]{0:T(512)}, f32[512]{0:T(512)S(1)}, u32[]{:S(2)}) copy-start(f32[512]{0:T(512)S(1)} %convert_element_type.233) | copy-start | bytes 6148
  201.2 22.9 %copy-start.10 = (s32[12,50,2,8]{1,2,3,0:T(2,128)}, s32[12,50,2,8]{1,2,3,0:T(2,128)S(1)}, u32[]{:S(2)}) copy-start(s32[12,50,2,8]{1,2,3,0:T(2,128)S(1)} %copy.246) | copy-start | bytes 115204
  241.1 23.2 %all-to-all-start.2 = ((bf16[8,168,512]{2,1,0:T(8,128)(2,1)}), bf16[8,168,512]{2,1,0:T(8,128)(2,1)}, u32[]{:S(2)}, u32[]{:S(2)}) async-start(bf16[8,168,512]{2,1,0:T(8,128)(2,1)} %copy.249), calls=%async_computation.2 | async-start | bytes 2752512 | tf_op jit(solution)/shard_map/all_to_all | solution.py:26
  308.8 26.4 %copy-start.42 = (pred[50]{0:T(512)(128)(4,1)S(1)}, pred[50]{0:T(512)(128)(4,1)}, u32[]{:S(2)}) copy-start(pred[50]{0:T(512)(128)(4,1)} %copy-done.41) | copy-start | bytes 154
  308.8 37.1 %all-to-all-start.3 = ((bf16[8,2,43008]{2,1,0:T(2,128)(2,1)}), bf16[8,2,43008]{2,1,0:T(2,128)(2,1)}, u32[]{:S(2)}, u32[]{:S(2)}) async-start(bf16[8,2,43008]{2,1,0:T(2,128)(2,1)} %reshape.422), calls=%async_computation.3 | async-start | bytes 2752512 | tf_op jit(solution)/shard_map/all_to_all | solution.py:30
  380.4 23.3 %all-to-all-start.4 = ((bf16[8,168,512]{2,1,0:T(8,128)(2,1)}), bf16[8,168,512]{2,1,0:T(8,128)(2,1)}, u32[]{:S(2)}, u32[]{:S(2)}) async-start(bf16[8,168,512]{2,1,0:T(8,128)(2,1)} %copy.258), calls=%async_computation.4 | async-start | bytes 2752512 | tf_op jit(solution)/shard_map/all_to_all | solution.py:26
  384.8 265.8 %reduce-scatter.16.cloned.1.call-start = ((), (), s32[]{:S(2)}) async-start(), calls=%async_computation.20 | async-start | bytes 147456
  447.5 23.2 %all-to-all-start.5 = ((bf16[8,2,43008]{2,1,0:T(2,128)(2,1)}), bf16[8,2,43008]{2,1,0:T(2,128)(2,1)}, u32[]{:S(2)}, u32[]{:S(2)}) async-start(bf16[8,2,43008]{2,1,0:T(2,128)(2,1)} %reshape.424), calls=%async_computation.5 | async-start | bytes 2752512 | tf_op jit(solution)/shard_map/all_to_all | solution.py:30
  451.8 199.6 %reduce-scatter.10.cloned.1.call-start = ((), (), s32[]{:S(2)}) async-start(), calls=%async_computation.17 | async-start | bytes 2621440 | tf_op jit(solution)/shard_map/reduce_scatter | solution.py:340
  508.0 18.5 %all-to-all-start.6 = ((bf16[4,2,38400]{2,1,0:T(2,128)(2,1)}), bf16[4,2,38400]{2,1,0:T(2,128)(2,1)S(1)}, u32[]{:S(2)}, u32[]{:S(2)}) async-start(bf16[4,2,38400]{2,1,0:T(2,128)(2,1)} %reshape.426), calls=%async_computation.6 | async-start | bytes 1228800 | tf_op jit(solution)/shard_map/all_to_all | solution.py:18
  513.0 140.6 %reduce-scatter.8.cloned.1.call-start = ((), (), s32[]{:S(2)}) async-start(), calls=%async_computation.16 | async-start | bytes 2621440 | tf_op jit(solution)/shard_map/reduce_scatter | solution.py:337
  563.3 43.9 %all-to-all-start.7 = ((bf16[4,2,115200]{2,1,0:T(2,128)(2,1)}), bf16[4,2,115200]{2,1,0:T(2,128)(2,1)}, u32[]{:S(2)}, u32[]{:S(2)}) async-start(bf16[4,2,115200]{2,1,0:T(2,128)(2,1)} %reshape.428), calls=%async_computation.7 | async-start | bytes 3686400 | tf_op jit(solution)/shard_map/all_to_all | solution.py:22
  567.7 123.4 %reduce-scatter.14.cloned.1.call-start = ((), (), s32[]{:S(2)}) async-start(), calls=%async_computation.19 | async-start | bytes 589824 | tf_op jit(solution)/shard_map/reduce_scatter | solution.py:323
  570.4 120.8 %reduce-scatter.12.cloned.1.call-start = ((), (), s32[]{:S(2)}) async-start(), calls=%async_computation.18 | async-start | bytes 1769472 | tf_op jit(solution)/shard_map/reduce_scatter | solution.py:320
  648.5 79.8 %all-reduce.14.cloned.1.call-start = ((), (), s32[]{:S(2)}) async-start(), calls=%async_computation.21 | async-start | bytes 524288 | tf_op jit(solution)/shard_map/psum | solution.py:307
  655.7 32.7 %copy-start.25 = (f32[600]{0:T(1024)S(1)}, f32[600]{0:T(1024)}, u32[]{:S(2)}) copy-start(f32[600]{0:T(1024)} %copy-done.24) | copy-start | bytes 7204
  (46 other events, 194.7 us)
Sparse Core Ops, SparseCore 0:
  9.9 28.4 all-gather.4
  40.0 65.1 all-gather.6
  106.7 52.5 all-gather.8
  390.6 35.0 reduce-scatter.15
  459.8 45.5 reduce-scatter.9
  521.4 43.4 reduce-scatter.7
  572.0 36.7 reduce-scatter.13
  648.7 41.6 reduce-scatter.11
  692.8 35.4 all-reduce.13
where the time goes:
time: 741 us; the launch traced here: 738 us
  local copies, waits for them, and re-layouts  247 us (33%)
  waiting for transfers between devices  210 us (28%)
  matrix products  87 us (12%)
  blocking collectives  84.5 us (11%)
  other arithmetic  57.3 us (8%)
  starting transfers between devices  36.2 us (5%)
  between operations  16.4 us (2%)
    all_to_all x2, waiting for transfers between devices, regroup_heads(): lax.all_to_all(values, 'seq', split_axis=3, concat_axis=1, tiled=True)  86.8 us
    unnamed x137, local copies, waits for them, and re-layouts  60.1 us
    psum x1, waiting for transfers between devices, local(): lax.psum(dense_grads[2].astype(jnp.bfloat16), 'seq').astype(jnp.float32)  34.4 us
    all_to_all x2, waiting for transfers between devices, regroup_slots(): lax.all_to_all(values, 'seq', split_axis=1, concat_axis=3, tiled=True)  34 us
    all_to_all x4, local copies, waits for them, and re-layouts, regroup_slots(): lax.all_to_all(values, 'seq', split_axis=1, concat_axis=3, tiled=True)  33.6 us
    all_to_all x5, local copies, waits for them, and re-layouts, regroup_heads(): lax.all_to_all(values, 'seq', split_axis=3, concat_axis=1, tiled=True)  33.5 us
    all_to_all x2, waiting for transfers between devices, send_experts(): return lax.all_to_all(values, 'dp', split_axis=0, concat_axis=1, tiled=True)  32.1 us
    unnamed x2, blocking collectives  32 us
  transfers between devices with their start and end apart: 17, of which 8 were waited for; matrix products, arithmetic and copies ran while one was open for 43% of the time, Pallas kernels for 0%

commit v1 on v0

--- a/solution.py
+++ b/solution.py
@@ -1,6 +1,10 @@
+import functools
+
 import jax
 import jax.numpy as jnp
 from jax import lax
+from jax.experimental import pallas as pl
+from jax.experimental.pallas import tpu as pltpu
 from jax.sharding import PartitionSpec as P
 
 H = 8
@@ -85,7 +89,7 @@
     return total_rows
 
 
-def local(
+def by_heads(
     tokens,
     ln1_gain,
     ln1_bias,
@@ -357,6 +361,925 @@
     )
 
 
+BF = jnp.bfloat16
+F32 = jnp.float32
+MESH_ID = pl.DeviceIdType.MESH
+NEG = -1e30
+BP = 64
+VMEM_LIMIT = 64 * 1000 * 1024
+
+
+def nn(a, b):
+    return lax.dot_general(a, b, (((1,), (0,)), ((), ())), preferred_element_type=F32)
+
+
+def nt(a, b):
+    return lax.dot_general(a, b, (((1,), (1,)), ((), ())), preferred_element_type=F32)
+
+
+def tn(a, b):
+    return lax.dot_general(a, b, (((0,), (0,)), ((), ())), preferred_element_type=F32)
+
+
+def remote(src, dst, send_sem, recv_sem, dp, z):
+    return pltpu.make_async_remote_copy(
+        src_ref=src,
+        dst_ref=dst,
+        send_sem=send_sem,
+        recv_sem=recv_sem,
+        device_id=(dp, z),
+        device_id_type=MESH_ID,
+    )
+
+
+def entry_barrier(me, z, n_dp, n_z, use_dp, use_z):
+    barrier = pltpu.get_barrier_semaphore()
+    count = 0
+    if use_dp:
+        for k in range(1, n_dp):
+            pl.semaphore_signal(
+                barrier, inc=1, device_id=(lax.rem(me + k, n_dp), z), device_id_type=MESH_ID
+            )
+            count += 1
+    if use_z:
+        for k in range(1, n_z):
+            pl.semaphore_signal(
+                barrier, inc=1, device_id=(me, lax.rem(z + k, n_z)), device_id_type=MESH_ID
+            )
+            count += 1
+    pl.semaphore_wait(barrier, count)
+
+
+def rows_of(index, size):
+    return pl.ds(pl.multiple_of(index * size, size), size)
+
+
+def norm_parts(x):
+    centre = x - jnp.mean(x, axis=-1, keepdims=True)
+    scale = lax.rsqrt(jnp.mean(centre * centre, axis=-1, keepdims=True) + 1e-06)
+    return centre * scale, scale
+
+
+def norm_back(grad_hat, hat, scale):
+    return scale * (
+        grad_hat
+        - jnp.mean(grad_hat, axis=-1, keepdims=True)
+        - hat * jnp.mean(grad_hat * hat, axis=-1, keepdims=True)
+    )
+
+
+def half_masks():
+    lane = lax.broadcasted_iota(jnp.int32, (1, 128), 1)
+    low = jnp.where(lane < 64, 1.0, 0.0).astype(BF)
+    high = jnp.where(lane < 64, 0.0, 1.0).astype(BF)
+    return (low, high)
+
+
+def key_mask(z_blocks, block):
+    lane = lax.broadcasted_iota(jnp.int32, (1, z_blocks * BP), 1)
+    return (lane % BP < block) & ((lane // BP) * block + lane % BP < VALID)
+
+
+def row_mask(z_blocks, block):
+    row = lax.broadcasted_iota(jnp.int32, (z_blocks * BP, 1), 0)
+    return (row % BP < block) & ((row // BP) * block + row % BP < VALID)
+
+
+def gather_step(step, z, n_z, me, sends):
+    @pl.when(z >= step)
+    def _():
+        for full, send_sem, recv_sem in sends:
+            slot = z - step
+            remote(full.at[slot], full.at[slot], send_sem.at[0, step], recv_sem.at[slot], me, z).wait_recv()
+
+            @pl.when(z < n_z - 1)
+            def _():
+                remote(
+                    full.at[slot], full.at[slot], send_sem.at[0, step], recv_sem.at[slot], me, z + 1
+                ).start()
+
+    @pl.when(z + step < n_z)
+    def _():
+        for full, send_sem, recv_sem in sends:
+            slot = z + step
+            remote(full.at[slot], full.at[slot], send_sem.at[1, step], recv_sem.at[slot], me, z).wait_recv()
+
+            @pl.when(z > 0)
+            def _():
+                remote(
+                    full.at[slot], full.at[slot], send_sem.at[1, step], recv_sem.at[slot], me, z - 1
+                ).start()
+
+
+def gather_sends_done(z, n_z, me, sends):
+    for step in range(n_z):
+
+        @pl.when((z >= step) & (z < n_z - 1))
+        def _():
+            for full, send_sem, recv_sem in sends:
+                remote(
+                    full.at[0], full.at[0], send_sem.at[0, step], recv_sem.at[0], me, z
+                ).wait_send()
+
+        @pl.when((z + step < n_z) & (z > 0))
+        def _():
+            for full, send_sem, recv_sem in sends:
+                remote(
+                    full.at[0], full.at[0], send_sem.at[1, step], recv_sem.at[0], me, z
+                ).wait_send()
+
+
+def front_kernel(
+    dims,
+    tok, rts, wq, wo, vec, win, wout,
+    recv, win_all, wout_all, wq_all, wo_all, vsum, xpad, x2s, n2s, qkvs, outs, gts, meta, metat, lses,
+    xin, rin, vec_all, sbuf,
+    tok_ss, tok_rs, rts_ss, rts_rs, den_ss, den_rs, fwd_ss, win_ss, win_rs, wout_ss, wout_rs,
+    row_ss, row_rs, loc_sem,
+):
+    n_dp, n_z, im, block, cap, er = dims
+    me, z = lax.axis_index("dp"), lax.axis_index("seq")
+    sp = n_z * BP
+    half = n_dp // 2
+    entry_barrier(me, z, n_dp, n_z, True, True)
+    for k in range(1, n_z):
+        peer = lax.rem(z + k, n_z)
+        remote(tok.at[pl.ds(peer * im, im)], xin.at[z], tok_ss.at[k], tok_rs.at[z], me, peer).start()
+        remote(rts.at[pl.ds(peer * im, im)], rin.at[z], rts_ss.at[k], rts_rs.at[z], me, peer).start()
+    core, chip = lax.rem(me, 2), me // 2
+    partner = chip * 2 + 1 - core
+    dense = ((wq, wq_all, 64), (wo, wo_all, 64))
+    own_copies = [
+        pltpu.make_async_copy(tok.at[pl.ds(z * im, im)], xin.at[z], loc_sem.at[0]),
+        pltpu.make_async_copy(rts.at[pl.ds(z * im, im)], rin.at[z], loc_sem.at[1]),
+        pltpu.make_async_copy(win, win_all.at[z], loc_sem.at[2]),
+        pltpu.make_async_copy(wout, wout_all.at[z], loc_sem.at[3]),
+        pltpu.make_async_copy(wq, wq_all.at[rows_of(me, 64)], loc_sem.at[4]),
+        pltpu.make_async_copy(wo, wo_all.at[rows_of(me, 64)], loc_sem.at[5]),
+        pltpu.make_async_copy(vec, vec_all.at[me], loc_sem.at[6]),
+    ]
+    for copy in own_copies:
+        copy.start()
+
+    def dense_slot(array, index):
+        if array == 0:
+            return wq_all.at[rows_of(index, 64)]
+        if array == 1:
+            return wo_all.at[rows_of(index, 64)]
+        return vec_all.at[index]
+
+    dense_in = (wq, wo, vec)
+    for array in range(3):
+        for k in range(1, half):
+            peer = lax.rem(chip + k, half) * 2 + core
+            remote(
+                dense_in[array], dense_slot(array, me), den_ss.at[array, k], den_rs.at[array, me], peer, z
+            ).start()
+        remote(
+            dense_in[array], dense_slot(array, me), den_ss.at[array, 0], den_rs.at[array, me], partner, z
+        ).start()
+    sends = ((win_all, win_ss, win_rs), (wout_all, wout_ss, wout_rs))
+    for source, (full, send_sem, recv_sem) in zip((win, wout), sends):
+
+        @pl.when(z < n_z - 1)
+        def _():
+            remote(source, full.at[z], send_sem.at[0, 0], recv_sem.at[z], me, z + 1).start()
+
+        @pl.when(z > 0)
+        def _():
+            remote(source, full.at[z], send_sem.at[1, 0], recv_sem.at[z], me, z - 1).start()
+
+    xpad[...] = jnp.zeros_like(xpad)
+    for k in range(1, half):
+        origin = lax.rem(chip + k, half) * 2 + core
+        for array in range(3):
+            slot = dense_slot(array, origin)
+            remote(slot, slot, den_ss.at[array, 0], den_rs.at[array, origin], me, z).wait_recv()
+            remote(slot, slot, fwd_ss.at[array, k], den_rs.at[array, origin], partner, z).start()
+    for k in range(half):
+        origin = lax.rem(chip + k, half) * 2 + 1 - core
+        for array in range(3):
+            slot = dense_slot(array, origin)
+            remote(slot, slot, den_ss.at[array, 0], den_rs.at[array, origin], me, z).wait_recv()
+    for copy in own_copies:
+        copy.wait()
+    total = vec_all[0].astype(F32)
+    for k in range(1, n_dp):
+        total = total + vec_all[k].astype(F32)
+    vsum[...] = total
+    for k in range(1, n_z):
+        origin = lax.rem(z + k, n_z)
+        remote(xin.at[origin], xin.at[origin], tok_ss.at[0], tok_rs.at[origin], me, z).wait_recv()
+        remote(rin.at[origin], rin.at[origin], rts_ss.at[0], rts_rs.at[origin], me, z).wait_recv()
+
+    masks = half_masks()
+    keys_ok = key_mask(n_z, block)
+    gain_one, bias_one = vsum[0:1, :], vsum[1:2, :]
+    gain_two, bias_two = vsum[2:3, :], vsum[3:4, :]
+    router_t = vsum[8:16, :].astype(BF)
+    lane_low = lax.broadcasted_iota(jnp.int32, (sp, 128), 1) < 64
+    lane_id = lax.broadcasted_iota(jnp.int32, (sp, 128), 1)
+    before = lax.broadcasted_iota(jnp.int32, (sp, sp), 0)
+    after = lax.broadcasted_iota(jnp.int32, (sp, sp), 1)
+    prefix = jnp.where((before < after) & (before // BP == after // BP), 1.0, 0.0).astype(BF)
+    expert_id = lax.broadcasted_iota(jnp.int32, (8, sp), 0)
+    slot_lane = lax.broadcasted_iota(jnp.int32, (8, sp), 1)
+
+    def image(i, carry):
+        for b in range(n_z):
+            xpad[i, b * BP : b * BP + block, :] = xin[b, i]
+        x = xpad[i].astype(F32)
+        hat, _ = norm_parts(x)
+        normed = (hat * gain_one + bias_one).astype(BF)
+        qkvs[i] = nn(normed, wq_all[...]).astype(BF)
+        lse_all = jnp.zeros((sp, 128), F32)
+        for pair in range(4):
+            q2 = qkvs[i, :, pair * 128 : pair * 128 + 128]
+            k2 = qkvs[i, :, 512 + pair * 128 : 512 + pair * 128 + 128]
+            v2 = qkvs[i, :, 1024 + pair * 128 : 1024 + pair * 128 + 128]
+            parts = []
+            for side in range(2):
+                scores = nt(q2 * masks[side], k2) * 0.125
+                scores = jnp.where(keys_ok, scores, NEG)
+                top = jnp.max(scores, axis=-1, keepdims=True)
+                exponent = jnp.exp(scores - top)
+                whole = jnp.sum(exponent, axis=-1, keepdims=True)
+                lse_all = jnp.where(lane_id == pair * 2 + side, top + jnp.log(whole), lse_all)
+                parts.append(nn((exponent / whole).astype(BF), v2))
+            outs[i, :, pair * 128 : pair * 128 + 128] = jnp.where(lane_low, parts[0], parts[1]).astype(BF)
+        lses[i] = lse_all
+        x2 = x + nn(outs[i], wo_all[...])
+        x2s[i] = x2
+        hat2, _ = norm_parts(x2)
+        n2 = (hat2 * gain_two + bias_two).astype(BF)
+        n2s[i] = n2
+        logits = nt(router_t, n2)
+        raised = jnp.exp(logits - jnp.max(logits, axis=0, keepdims=True))
+        share = raised / jnp.sum(raised, axis=0, keepdims=True)
+        gts[i] = share
+        lane8 = lax.broadcasted_iota(jnp.int32, (8, 128), 1)
+        wide = jnp.concatenate([rin[0, i] + rin[1, i], rin[2, i] + rin[3, i]], axis=1)
+        hits = [(expert_id + 1) == wide[j : j + 1, :] for j in range(2)]
+        any_hit = jnp.where(hits[0] | hits[1], 1.0, 0.0)
+        place = nn(any_hit.astype(BF), prefix)
+        base = place + (expert_id * er + (slot_lane // BP) * cap + i * (n_z * cap) + 1).astype(F32)
+        lines = [jnp.sum(jnp.where(hit, base, 0.0), axis=0, keepdims=True) - 1.0 for hit in hits]
+        lines += [jnp.sum(jnp.where(hit, share, 0.0), axis=0, keepdims=True) for hit in hits]
+        table = jnp.concatenate(lines + [jnp.zeros((124, sp), F32)], axis=0)
+        meta[i] = table[0:8]
+        metat[i] = jnp.transpose(table)
+        return carry
+
+    lax.fori_loop(0, im, image, 0)
+
+    row_id = lax.broadcasted_iota(jnp.int32, (er, sp), 0)
+    for k in range(n_dp):
+        peer = lax.rem(me + k, n_dp)
+        want = (row_id + peer * er).astype(F32)
+        total = jnp.zeros((er, 512), F32)
+        for i in range(im):
+            pick = (want == meta[i, 0:1, :]) | (want == meta[i, 1:2, :])
+            total = total + nn(jnp.where(pick, 1.0, 0.0).astype(BF), n2s[i])
+        if k == 0:
+            recv[rows_of(me, er)] = total.astype(BF)
+        else:
+            sbuf[k] = total.astype(BF)
+            remote(
+                sbuf.at[k], recv.at[rows_of(me, er)], row_ss.at[k], row_rs.at[me], peer, z
+            ).start()
+    for step in range(1, n_z):
+        gather_step(step, z, n_z, me, sends)
+    for k in range(1, n_dp):
+        origin = lax.rem(me + k, n_dp)
+        spot = recv.at[rows_of(origin, er)]
+        remote(spot, spot, row_ss.at[0], row_rs.at[origin], me, z).wait_recv()
+    gather_sends_done(z, n_z, me, sends)
+    for k in range(1, n_dp):
+        remote(sbuf.at[k], sbuf.at[k], row_ss.at[k], row_rs.at[0], me, z).wait_send()
+    for k in range(1, n_z):
+        remote(xin.at[0], xin.at[0], tok_ss.at[k], tok_rs.at[0], me, z).wait_send()
+        remote(rin.at[0], rin.at[0], rts_ss.at[k], rts_rs.at[0], me, z).wait_send()
+    for array in range(3):
+        for k in range(half):
+            remote(
+                dense_in[array], dense_in[array], den_ss.at[array, k], den_rs.at[array, 0], me, z
+            ).wait_send()
+        for k in range(1, half):
+            remote(
+                dense_in[array], dense_in[array], fwd_ss.at[array, k], den_rs.at[array, 0], me, z
+            ).wait_send()
+
+
+GELU_C = 0.7978845608028654
+GELU_K = 0.044715
+
+
+def expert_kernel(
+    dims,
+    rows, win_all, wout_all, tgt,
+    ret, acts, slopes, tin,
+    ubuf,
+    u_ss, u_rs, tgt_ss, tgt_rs, loc_sem,
+):
+    n_dp, n_z, im, block, cap, er = dims
+    me, z = lax.axis_index("dp"), lax.axis_index("seq")
+    entry_barrier(me, z, n_dp, n_z, True, True)
+    for k in range(1, n_z):
+        peer = lax.rem(z + k, n_z)
+        remote(tgt.at[pl.ds(peer * im, im)], tin.at[z], tgt_ss.at[k], tgt_rs.at[z], me, peer).start()
+    own = pltpu.make_async_copy(tgt.at[pl.ds(z * im, im)], tin.at[z], loc_sem)
+    own.start()
+    two = 2 * er
+
+    def hidden(step, carry):
+        shard, chunk = step // 8, lax.rem(step, 8)
+        part, side = chunk // 2, lax.rem(chunk, 2)
+        x = rows[rows_of(part, two)]
+        for side in range(2):
+            pre = nn(x, win_all[shard, :, side * 256 : side * 256 + 256])
+            square = pre * pre
+            tanh = jnp.tanh(pre * (GELU_C + (GELU_C * GELU_K) * square))
+            gate = 0.5 + 0.5 * tanh
+            acts[shard, rows_of(part, two), side * 256 : side * 256 + 256] = (pre * gate).astype(BF)
+            slope = gate + pre * (0.5 - 0.5 * tanh * tanh) * (
+                GELU_C + (3.0 * GELU_C * GELU_K) * square
+            )
+            slopes[shard, rows_of(part, two), side * 256 : side * 256 + 256] = slope.astype(BF)
+        return carry
+
+    def hidden_step(step, carry):
+        return hidden((step // 4) * 8 + lax.rem(step, 4) * 2, carry)
+
+    lax.fori_loop(0, 4 * n_z, hidden_step, 0)
+    for k in range(n_dp // 2):
+        part = lax.rem(me // 2 + k, n_dp // 2)
+        total = jnp.zeros((two, 512), F32)
+        for shard in range(n_z):
+            total = total + nn(acts[shard, rows_of(part, two)], wout_all[shard])
+        out = total.astype(BF)
+        if k == 0:
+            ubuf[0] = out[0:er]
+            ubuf[1] = out[er:two]
+            mine = lax.rem(me, 2)
+            peer = (me // 2) * 2 + 1 - mine
+            ret[rows_of(me, er)] = ubuf[mine]
+            remote(
+                ubuf.at[1 - mine], ret.at[rows_of(me, er)], u_ss.at[1], u_rs.at[me], peer, z
+            ).start()
+        else:
+            for c in range(2):
+                ubuf[2 * k + c] = out[c * er : c * er + er]
+                remote(
+                    ubuf.at[2 * k + c],
+                    ret.at[rows_of(me, er)],
+                    u_ss.at[2 * k + c],
+                    u_rs.at[me],
+                    part * 2 + c,
+                    z,
+                ).start()
+    for k in range(1, n_dp):
+        origin = lax.rem(me + k, n_dp)
+        spot = ret.at[rows_of(origin, er)]
+        remote(spot, spot, u_ss.at[0], u_rs.at[origin], me, z).wait_recv()
+    for k in range(1, n_dp):
+        remote(ubuf.at[k], ubuf.at[k], u_ss.at[k], u_rs.at[0], me, z).wait_send()
+    own.wait()
+    for k in range(1, n_z):
+        origin = lax.rem(z + k, n_z)
+        remote(tin.at[origin], tin.at[origin], tgt_ss.at[0], tgt_rs.at[origin], me, z).wait_recv()
+    for k in range(1, n_z):
+        remote(tin.at[0], tin.at[0], tgt_ss.at[k], tgt_rs.at[0], me, z).wait_send()
+
+
+def mix_kernel(
+    dims,
+    ret, tin, x2s, n2s, meta, metat, gts,
+    recv, mixed, dys, dlogs, grouter,
+    mbuf, dus, sbuf,
+    row_ss, row_rs, mix_ss, mix_rs, loc_sem,
+):
+    n_dp, n_z, im, block, cap, er = dims
+    me, z = lax.axis_index("dp"), lax.axis_index("seq")
+    sp = n_z * BP
+    nr = n_dp * er
+    entry_barrier(me, z, n_dp, n_z, True, True)
+    rows_ok = row_mask(n_z, block)
+    line = lax.broadcasted_iota(jnp.int32, (sp, nr), 1).astype(F32)
+    lane_id = lax.broadcasted_iota(jnp.int32, (sp, 128), 1)
+
+    def image(i, carry):
+        cols = metat[i]
+        picked = []
+        for j in range(2):
+            pick = jnp.where(line == cols[:, j : j + 1], 1.0, 0.0).astype(BF)
+            picked.append(nn(pick, ret[...]))
+        mix = x2s[i] + cols[:, 2:3] * picked[0] + cols[:, 3:4] * picked[1]
+        mix_b = mix.astype(BF)
+        for b in range(n_z):
+            mbuf[b, i] = mix_b[b * BP : b * BP + block]
+        for b in range(n_z):
+            dys[i, b * BP : b * BP + block, :] = tin[b, i].astype(F32)
+        dy = jnp.where(rows_ok, mix - dys[i], 0.0)
+        dys[i] = dy
+        dus[0, i] = (cols[:, 2:3] * dy).astype(BF)
+        dus[1, i] = (cols[:, 3:4] * dy).astype(BF)
+        slope = jnp.where(
+            lane_id == 0, jnp.sum(dy * picked[0], axis=-1, keepdims=True), 0.0
+        ) + jnp.where(lane_id == 1, jnp.sum(dy * picked[1], axis=-1, keepdims=True), 0.0)
+        dlogs[i] = slope
+        return carry
+
+    lax.fori_loop(0, im, image, 0)
+    row_id = lax.broadcasted_iota(jnp.int32, (er, sp), 0)
+    for k in range(n_dp):
+        peer = lax.rem(me + k, n_dp)
+        want = (row_id + peer * er).astype(F32)
+        total = jnp.zeros((er, 512), F32)
+        for i in range(im):
+            for j in range(2):
+                pick = jnp.where(want == meta[i, j : j + 1, :], 1.0, 0.0).astype(BF)
+                total = total + nn(pick, dus[j, i])
+        if k == 0:
+            recv[rows_of(me, er)] = total.astype(BF)
+        else:
+            sbuf[k] = total.astype(BF)
+            remote(
+                sbuf.at[k], recv.at[rows_of(me, er)], row_ss.at[k], row_rs.at[me], peer, z
+            ).start()
+    for k in range(1, n_z):
+        peer = lax.rem(z + k, n_z)
+        remote(mbuf.at[peer], mixed.at[pl.ds(z * im, im)], mix_ss.at[k], mix_rs.at[z], me, peer).start()
+    own = pltpu.make_async_copy(mbuf.at[z], mixed.at[pl.ds(z * im, im)], loc_sem)
+    own.start()
+    expert_id = lax.broadcasted_iota(jnp.int32, (8, sp), 0).astype(F32)
+    router = jnp.zeros((8, 512), F32)
+    for i in range(im):
+        flat = jnp.transpose(dlogs[i])
+        at = [meta[i, j : j + 1, :] for j in range(2)]
+        share = gts[i]
+        grad = jnp.zeros((8, sp), F32)
+        for j in range(2):
+            inside = (at[j] >= expert_id * er) & (at[j] < expert_id * er + er)
+            grad = grad + jnp.where(inside, flat[j : j + 1, :], 0.0)
+        inner = jnp.sum(share * grad, axis=0, keepdims=True)
+        dlog = (share * (grad - inner)).astype(BF)
+        dlogs[i, 0:8, 0:128] = dlog[:, 0:128].astype(F32)
+        dlogs[i, 8:16, 0:128] = dlog[:, 128:256].astype(F32)
+        router = router + nn(dlog, n2s[i])
+    grouter[...] = router
+    for k in range(1, n_dp):
+        origin = lax.rem(me + k, n_dp)
+        spot = recv.at[rows_of(origin, er)]
+        remote(spot, spot, row_ss.at[0], row_rs.at[origin], me, z).wait_recv()
+    for k in range(1, n_dp):
+        remote(sbuf.at[k], sbuf.at[k], row_ss.at[k], row_rs.at[0], me, z).wait_send()
+    own.wait()
+    for k in range(1, n_z):
+        origin = lax.rem(z + k, n_z)
+        spot = mixed.at[pl.ds(origin * im, im)]
+        remote(spot, spot, mix_ss.at[0], mix_rs.at[origin], me, z).wait_recv()
+    for k in range(1, n_z):
+        remote(mbuf.at[0], mbuf.at[0], mix_ss.at[k], mix_rs.at[0], me, z).wait_send()
+
+
+def expert_back_kernel(
+    dims,
+    rows, drows, acts, slopes, win_all, wout_all,
+    ret, dws,
+    dpres, ubuf,
+    u_ss, u_rs,
+):
+    n_dp, n_z, im, block, cap, er = dims
+    me, z = lax.axis_index("dp"), lax.axis_index("seq")
+    entry_barrier(me, z, n_dp, n_z, True, False)
+    two = 2 * er
+    for k in range(n_dp // 2):
+        part = lax.rem(me // 2 + k, n_dp // 2)
+        at = rows_of(part, two)
+        du = drows[at]
+        total = jnp.zeros((two, 512), F32)
+        for shard in range(n_z):
+            dpre = (nt(du, wout_all[shard]) * slopes[shard, at].astype(F32)).astype(BF)
+            dpres[shard, at] = dpre
+            total = total + nt(dpre, win_all[shard])
+        out = total.astype(BF)
+        if k == 0:
+            ubuf[0] = out[0:er]
+            ubuf[1] = out[er:two]
+            mine = lax.rem(me, 2)
+            peer = (me // 2) * 2 + 1 - mine
+            ret[rows_of(me, er)] = ubuf[mine]
+            remote(
+                ubuf.at[1 - mine], ret.at[rows_of(me, er)], u_ss.at[1], u_rs.at[me], peer, z
+            ).start()
+        else:
+            for c in range(2):
+                ubuf[2 * k + c] = out[c * er : c * er + er]
+                remote(
+                    ubuf.at[2 * k + c],
+                    ret.at[rows_of(me, er)],
+                    u_ss.at[2 * k + c],
+                    u_rs.at[me],
+                    part * 2 + c,
+                    z,
+                ).start()
+
+    def weights(shard, carry):
+        dws[shard, 0:512, :] = tn(rows[...], dpres[shard]).astype(BF)
+        dws[shard, 512:1024, :] = tn(acts[shard], drows[...]).astype(BF)
+        return carry
+
+    lax.fori_loop(0, n_z, weights, 0)
+    for k in range(1, n_dp):
+        origin = lax.rem(me + k, n_dp)
+        spot = ret.at[rows_of(origin, er)]
+        remote(spot, spot, u_ss.at[0], u_rs.at[origin], me, z).wait_recv()
+    for k in range(1, n_dp):
+        remote(ubuf.at[k], ubuf.at[k], u_ss.at[k], u_rs.at[0], me, z).wait_send()
+
+
+def back_kernel(
+    dims,
+    dret, dws, dys, dlogs, x2s, xpad, qkvs, outs, lses, metat, wq_all, wo_all, vsum,
+    gtok, gbig, gvec, gin, gout,
+    gacc, tbuf, from_left, from_right, to_right, to_left,
+    tok_ss, tok_rs, r_ss, r_rs, l_ss, l_rs, loc_sem,
+):
+    n_dp, n_z, im, block, cap, er = dims
+    me, z = lax.axis_index("dp"), lax.axis_index("seq")
+    sp = n_z * BP
+    nr = n_dp * er
+    entry_barrier(me, z, n_dp, n_z, False, True)
+    last = n_z - 1
+
+    def pass_right(target):
+        @pl.when(z < target)
+        def _():
+            @pl.when(z == 0)
+            def _():
+                remote(
+                    dws.at[target], from_left.at[target], r_ss.at[target], r_rs.at[target], me, z + 1
+                ).start()
+
+            @pl.when(z > 0)
+            def _():
+                here = from_left.at[target]
+                remote(here, here, r_ss.at[target], r_rs.at[target], me, z).wait_recv()
+
+                def add(c, carry):
+                    at = rows_of(c, 128)
+                    to_right[target, at] = (
+                        dws[target, at].astype(F32) + from_left[target, at].astype(F32)
+                    ).astype(BF)
+                    return carry
+
+                lax.fori_loop(0, 8, add, 0)
+                remote(
+                    to_right.at[target], here, r_ss.at[target], r_rs.at[target], me, z + 1
+                ).start()
+
+    def pass_left(target):
+        @pl.when(z > target)
+        def _():
+            @pl.when(z == last)
+            def _():
+                remote(
+                    dws.at[target], from_right.at[target], l_ss.at[target], l_rs.at[target], me, z - 1
+                ).start()
+
+            @pl.when(z < last)
+            def _():
+                here = from_right.at[target]
+                remote(here, here, l_ss.at[target], l_rs.at[target], me, z).wait_recv()
+
+                def add(c, carry):
+                    at = rows_of(c, 128)
+                    to_left[target, at] = (
+                        dws[target, at].astype(F32) + from_right[target, at].astype(F32)
+                    ).astype(BF)
+                    return carry
+
+                lax.fori_loop(0, 8, add, 0)
+                remote(
+                    to_left.at[target], here, l_ss.at[target], l_rs.at[target], me, z - 1
+                ).start()
+
+    def pass_on(step, first):
+        for way, target in ((pass_right, last - step), (pass_left, step)):
+            edge = 0 if way is pass_right else last
+
+            @pl.when((z == edge) if first else (z != edge))
+            def _():
+                way(target)
+
+    for step in range(n_z - 1):
+        pass_on(step, True)
+
+    masks = half_masks()
+    keys_ok = key_mask(n_z, block)
+    gain_one, bias_one = vsum[0:1, :], vsum[1:2, :]
+    gain_two = vsum[2:3, :]
+    router_t = vsum[8:16, :].astype(BF)
+    line = lax.broadcasted_iota(jnp.int32, (sp, nr), 1).astype(F32)
+    lane_low = lax.broadcasted_iota(jnp.int32, (sp, 128), 1) < 64
+    gacc[...] = jnp.zeros_like(gacc)
+    gvec[...] = jnp.zeros_like(gvec)
+
+    def image(i, carry):
+        cols = metat[i]
+        pick = jnp.where((line == cols[:, 0:1]) | (line == cols[:, 1:2]), 1.0, 0.0).astype(BF)
+        dlog = jnp.concatenate([dlogs[i, 0:8, :], dlogs[i, 8:16, :]], axis=1).astype(BF)
+        dn2 = nn(pick, dret[...]) + tn(dlog, router_t)
+        hat2, scale2 = norm_parts(x2s[i])
+        gvec[2:3, :] += jnp.sum(dn2 * hat2, axis=0, keepdims=True)
+        gvec[3:4, :] += jnp.sum(dn2, axis=0, keepdims=True)
+        dx2 = dys[i] + norm_back(dn2 * gain_two, hat2, scale2)
+        da = dx2.astype(BF)
+        gacc[:, 1536:2048] += tn(outs[i], da)
+        do = nt(da, wo_all[...]).astype(BF)
+        hat1, scale1 = norm_parts(xpad[i].astype(F32))
+        n1 = (hat1 * gain_one + bias_one).astype(BF)
+        dn1 = jnp.zeros((sp, 512), F32)
+        for pair in range(4):
+            at = pair * 128
+            q2 = qkvs[i, :, at : at + 128]
+            k2 = qkvs[i, :, 512 + at : 512 + at + 128]
+            v2 = qkvs[i, :, 1024 + at : 1024 + at + 128]
+            do2 = do[:, at : at + 128]
+            grads = ([], [], [])
+            for side in range(2):
+                head = pair * 2 + side
+                scores = nt(q2 * masks[side], k2) * 0.125
+                scores = jnp.where(keys_ok, scores, NEG)
+                prob = jnp.exp(scores - lses[i, :, head : head + 1])
+                dprob = nt(do2 * masks[side], v2)
+                inner = jnp.sum(prob * dprob, axis=-1, keepdims=True)
+                ds = (prob * (dprob - inner)).astype(BF)
+                grads[0].append(nn(ds, k2))
+                grads[1].append(tn(ds, q2))
+                grads[2].append(tn(prob.astype(BF), do2))
+            for part in range(3):
+                grad = jnp.where(lane_low, grads[part][0], grads[part][1])
+                if part < 2:
+                    grad = grad * 0.125
+                grad = grad.astype(BF)
+                col = part * 512 + at
+                gacc[:, col : col + 128] += tn(n1, grad)
+                dn1 = dn1 + nt(grad, wq_all[:, col : col + 128])
+        gvec[0:1, :] += jnp.sum(dn1 * hat1, axis=0, keepdims=True)
+        gvec[1:2, :] += jnp.sum(dn1, axis=0, keepdims=True)
+        dx = (dx2 + norm_back(dn1 * gain_one, hat1, scale1)).astype(BF)
+        for b in range(n_z):
+            tbuf[b, i] = dx[b * BP : b * BP + block]
+        return carry
+
+    lax.fori_loop(0, im, image, 0)
+    for k in range(1, n_z):
+        peer = lax.rem(z + k, n_z)
+        remote(tbuf.at[peer], gtok.at[pl.ds(z * im, im)], tok_ss.at[k], tok_rs.at[z], me, peer).start()
+    own = pltpu.make_async_copy(tbuf.at[z], gtok.at[pl.ds(z * im, im)], loc_sem)
+    own.start()
+    gbig[...] = gacc[...].astype(BF)
+    for step in range(n_z - 1):
+        pass_on(step, False)
+
+    @pl.when(z > 0)
+    def _():
+        here = from_left.at[z]
+        remote(here, here, r_ss.at[0], r_rs.at[z], me, z).wait_recv()
+
+    @pl.when(z < last)
+    def _():
+        here = from_right.at[z]
+        remote(here, here, l_ss.at[0], l_rs.at[z], me, z).wait_recv()
+
+    def finish(c, carry):
+        at = rows_of(c, 128)
+        left = jnp.where(z > 0, from_left[z, at].astype(F32), 0.0)
+        right = jnp.where(z < last, from_right[z, at].astype(F32), 0.0)
+        total = dws[z, at].astype(F32) + left + right
+
+        @pl.when(c < 4)
+        def _():
+            gin[at] = total
+
+        @pl.when(c >= 4)
+        def _():
+            gout[rows_of(c - 4, 128)] = total
+
+        return carry
+
+    lax.fori_loop(0, 8, finish, 0)
+    own.wait()
+    for k in range(1, n_z):
+        origin = lax.rem(z + k, n_z)
+        spot = gtok.at[pl.ds(origin * im, im)]
+        remote(spot, spot, tok_ss.at[0], tok_rs.at[origin], me, z).wait_recv()
+    for k in range(1, n_z):
+        remote(tbuf.at[0], tbuf.at[0], tok_ss.at[k], tok_rs.at[0], me, z).wait_send()
+    for target in range(n_z):
+
+        @pl.when(z < target)
+        def _():
+            remote(dws.at[0], dws.at[0], r_ss.at[target], r_rs.at[0], me, z).wait_send()
+
+        @pl.when(z > target)
+        def _():
+            remote(dws.at[0], dws.at[0], l_ss.at[target], l_rs.at[0], me, z).wait_send()
+
+
+def dense_kernel(
+    dims,
+    gbig, gvec,
+    big, small,
+    brecv, vrecv, bz, vz, bsend, vsend,
+    b_ss, b_rs, v_ss, v_rs, bz_ss, bz_rs, vz_ss, vz_rs,
+):
+    n_dp, n_z, im, block, cap, er = dims
+    me, z = lax.axis_index("dp"), lax.axis_index("seq")
+    entry_barrier(me, z, n_dp, n_z, True, True)
+    for k in range(1, n_dp):
+        peer = lax.rem(me + k, n_dp)
+        remote(gbig.at[rows_of(peer, 64)], brecv.at[me], b_ss.at[k], b_rs.at[me], peer, z).start()
+        remote(gvec, vrecv.at[me], v_ss.at[k], v_rs.at[me], peer, z).start()
+    total = gbig[rows_of(me, 64)].astype(F32)
+    vtotal = gvec[...].astype(F32)
+    for k in range(1, n_dp):
+        origin = lax.rem(me + k, n_dp)
+        remote(brecv.at[origin], brecv.at[origin], b_ss.at[0], b_rs.at[origin], me, z).wait_recv()
+        remote(vrecv.at[origin], vrecv.at[origin], v_ss.at[0], v_rs.at[origin], me, z).wait_recv()
+        total = total + brecv[origin].astype(F32)
+        vtotal = vtotal + vrecv[origin].astype(F32)
+    bsend[...] = total.astype(BF)
+    vsend[...] = vtotal.astype(BF)
+    for k in range(1, n_z):
+        peer = lax.rem(z + k, n_z)
+        remote(bsend, bz.at[z], bz_ss.at[k], bz_rs.at[z], me, peer).start()
+        remote(vsend, vz.at[z], vz_ss.at[k], vz_rs.at[z], me, peer).start()
+    for k in range(1, n_z):
+        origin = lax.rem(z + k, n_z)
+        remote(bz.at[origin], bz.at[origin], bz_ss.at[0], bz_rs.at[origin], me, z).wait_recv()
+        remote(vz.at[origin], vz.at[origin], vz_ss.at[0], vz_rs.at[origin], me, z).wait_recv()
+        total = total + bz[origin].astype(F32)
+        vtotal = vtotal + vz[origin].astype(F32)
+    big[...] = total
+    small[...] = vtotal
+    for k in range(1, n_dp):
+        remote(brecv.at[0], brecv.at[0], b_ss.at[k], b_rs.at[0], me, z).wait_send()
+        remote(vrecv.at[0], vrecv.at[0], v_ss.at[k], v_rs.at[0], me, z).wait_send()
+    for k in range(1, n_z):
+        remote(bsend, bsend, bz_ss.at[k], bz_rs.at[0], me, z).wait_send()
+        remote(vsend, vsend, vz_ss.at[k], vz_rs.at[0], me, z).wait_send()
+
+
+def call(kernel, dims, collective_id, outs, scratch, name, *args):
+    spec = pl.BlockSpec(memory_space=pltpu.VMEM)
+    return pl.pallas_call(
+        functools.partial(kernel, dims),
+        out_shape=[jax.ShapeDtypeStruct(shape, kind) for shape, kind in outs],
+        in_specs=[spec] * len(args),
+        out_specs=[spec] * len(outs),
+        scratch_shapes=scratch,
+        compiler_params=pltpu.CompilerParams(
+            collective_id=collective_id, has_side_effects=True, vmem_limit_bytes=VMEM_LIMIT
+        ),
+        name=name,
+    )(*args)
+
+
+def whole_images(
+    tokens, ln1_gain, ln1_bias, w_qkv, w_out, ln2_gain, ln2_bias, w_router, expert_in, expert_out, routes, targets
+):
+    n_dp, n_z = lax.axis_size("dp"), lax.axis_size("seq")
+    image_count, block, width = tokens.shape
+    im = image_count // n_z
+    cap = 2 * S // (n_z * w_router.shape[1]) + 2
+    er = -(-(im * n_z * cap) // 16) * 16
+    dims = (n_dp, n_z, im, block, cap, er)
+    sp, nr = n_z * BP, n_dp * er
+    me, z = lax.axis_index("dp"), lax.axis_index("seq")
+    dma, vm = pltpu.SemaphoreType.DMA, pltpu.VMEM
+
+    valid = z * block + jnp.arange(block) < VALID
+    lines = jnp.where(valid[None, None, :], jnp.transpose(routes, (0, 2, 1)) + 1, 0)
+    lines = jnp.pad(lines, ((0, 0), (0, 6), (0, BP - block)))
+    odd = lax.rem(z, 2) == 1
+    lines = jnp.concatenate([jnp.where(odd, 0, lines), jnp.where(odd, lines, 0)], axis=-1)
+    vec = jnp.concatenate(
+        [
+            jnp.stack([ln1_gain, ln1_bias, ln2_gain, ln2_bias]),
+            jnp.zeros((4, ln1_gain.shape[0]), BF),
+            jnp.transpose(w_router),
+        ],
+        axis=0,
+    )
+    vec = lax.dynamic_update_slice(jnp.zeros((16, width), BF), vec, (0, me * ln1_gain.shape[0]))
+
+    (recv, win_all, wout_all, wq_all, wo_all, vsum, xpad, x2s, n2s, qkvs, outs, gts, meta, metat, lses) = call(
+        front_kernel, dims, 1,
+        [
+            ((nr, width), BF), ((n_z, 512, 512), BF), ((n_z, 512, 512), BF), ((width, 1536), BF), ((width, width), BF),
+            ((16, width), F32), ((im, sp, width), BF), ((im, sp, width), F32), ((im, sp, width), BF),
+            ((im, sp, 1536), BF), ((im, sp, width), BF), ((im, 8, sp), F32), ((im, 8, sp), F32), ((im, sp, 128), F32),
+            ((im, sp, 128), F32),
+        ],
+        [
+            vm((n_z, im, block, width), BF), vm((n_z, im, 8, 128), jnp.int32), vm((n_dp, 16, width), BF),
+            vm((n_dp, er, width), BF),
+            dma((n_z,)), dma((n_z,)), dma((n_z,)), dma((n_z,)), dma((3, n_dp // 2)), dma((3, n_dp)), dma((3, n_dp // 2)),
+            dma((2, n_z)), dma((n_z,)), dma((2, n_z)), dma((n_z,)), dma((n_dp,)), dma((n_dp,)), dma((7,)),
+        ],
+        "front",
+        tokens, lines, w_qkv, w_out, vec, expert_in[0], expert_out[0],
+    )
+    ret, acts, slopes, tin = call(
+        expert_kernel, dims, 2,
+        [((nr, width), BF), ((n_z, nr, 512), BF), ((n_z, nr, 512), BF), ((n_z, im, block, width), BF)],
+        [vm((n_dp, er, width), BF), dma((n_dp,)), dma((n_dp,)), dma((n_z,)), dma((n_z,)), dma],
+        "experts",
+        recv, win_all, wout_all, targets,
+    )
+    drows, mixed, dys, dlogs, grouter = call(
+        mix_kernel, dims, 3,
+        [
+            ((nr, width), BF), ((image_count, block, width), BF), ((im, sp, width), F32), ((im, sp, 128), F32),
+            ((8, width), F32),
+        ],
+        [
+            vm((n_z, im, block, width), BF), vm((2, im, sp, width), BF), vm((n_dp, er, width), BF),
+            dma((n_dp,)), dma((n_dp,)), dma((n_z,)), dma((n_z,)), dma,
+        ],
+        "mix",
+        ret, tin, x2s, n2s, meta, metat, gts,
+    )
+    dret, dws = call(
+        expert_back_kernel, dims, 4,
+        [((nr, width), BF), ((n_z, 1024, 512), BF)],
+        [vm((n_z, nr, 512), BF), vm((n_dp, er, width), BF), dma((n_dp,)), dma((n_dp,))],
+        "experts_back",
+        recv, drows, acts, slopes, win_all, wout_all,
+    )
+    gtok, gbig, gvec, gin, gout = call(
+        back_kernel, dims, 5,
+        [
+            ((image_count, block, width), BF), ((width, 2048), BF), ((8, width), F32), ((512, 512), F32),
+            ((512, 512), F32),
+        ],
+        [
+            vm((width, 2048), F32), vm((n_z, im, block, width), BF), vm((n_z, 1024, 512), BF), vm((n_z, 1024, 512), BF),
+            vm((n_z, 1024, 512), BF), vm((n_z, 1024, 512), BF),
+            dma((n_z,)), dma((n_z,)), dma((n_z,)), dma((n_z,)), dma((n_z,)), dma((n_z,)), dma,
+        ],
+        "back",
+        dret, dws, dys, dlogs, x2s, xpad, qkvs, outs, lses, metat, wq_all, wo_all, vsum,
+    )
+    big, small = call(
+        dense_kernel, dims, 6,
+        [((64, 2048), F32), ((16, width), F32)],
+        [
+            vm((n_dp, 64, 2048), BF), vm((n_dp, 16, width), BF), vm((n_z, 64, 2048), BF), vm((n_z, 16, width), BF),
+            vm((64, 2048), BF), vm((16, width), BF),
+            dma((n_dp,)), dma((n_dp,)), dma((n_dp,)), dma((n_dp,)), dma((n_z,)), dma((n_z,)), dma((n_z,)), dma((n_z,)),
+        ],
+        "dense",
+        gbig, jnp.concatenate([gvec, grouter], axis=0).astype(BF),
+    )
+    part = lax.dynamic_slice(small, (0, me * ln1_gain.shape[0]), (16, ln1_gain.shape[0]))
+    return (
+        mixed,
+        gtok.astype(F32),
+        part[0],
+        part[1],
+        big[:, 0:1536],
+        big[:, 1536:2048],
+        part[2],
+        part[3],
+        jnp.transpose(part[8:16]),
+        gin[None],
+        gout[None],
+    )
+
+
+def fits(tokens, w_qkv, w_router, expert_in):
+    n_dp, n_z = lax.axis_size("dp"), lax.axis_size("seq")
+    return (
+        n_dp == 8
+        and n_z == 4
+        and tokens.shape[0] % n_z == 0
+        and tokens.shape[1] <= BP
+        and tokens.shape[2] == 512
+        and w_qkv.shape == (64, 1536)
+        and w_router.shape[1] == n_dp
+        and expert_in.shape == (1, 512, 512)
+    )
+
+
+def local(*args):
+    if fits(args[0], args[3], args[7], args[8]):
+        return whole_images(*args)
+    return by_heads(*args)
+
+
 def solution(mesh):
     placed = (
         P("dp", "seq", None),

time: 741 us -> 383 us (0.52)
  Pallas kernels: 0 us -> 362 us
  local copies, waits for them, and re-layouts: 247 us -> 11.1 us
  waiting for transfers between devices: 210 us -> 0 us
  matrix products: 87 us -> 0 us
  blocking collectives: 84.5 us -> 0 us
  other arithmetic: 57.3 us -> 4.03 us
  starting transfers between devices: 36.2 us -> 0 us
  between operations: 16.4 us -> 0.75 us
    pallas_call x0 -> x6, Pallas kernels: none -> 362 us  [call(): pl.pallas_call(functools.partial(kernel, dims), out_shape=[jax.ShapeDtype...]
    all_to_all x8 -> x0, waiting for transfers between devices: 164 us -> none  [the longest x2 86.8 us: regroup_heads(): lax.all_to_all(values, 'seq', split_axis=3, concat_axis=1, tiled=True)]
    all_to_all x11 -> x0, local copies, waits for them, and re-layouts: 87.7 us -> none  [the longest x4 33.6 us: regroup_slots(): lax.all_to_all(values, 'seq', split_axis=1, concat_axis=3, tiled=True)]
    dot_general x25 -> x0, matrix products: 87 us -> none  [the longest x1 12.5 us: expert_back(): jnp.einsum('erd,efd->erf', grad_piece, back_out, preferred_element_type=j...]
    unnamed x137 -> x15, local copies, waits for them, and re-layouts: 60.1 us -> 3.41 us
    all_gather x2 -> x0, blocking collectives: 44 us -> none  [the longest x1 22.7 us: local(): lax.all_gather(w_out, 'dp', axis=0, tiled=True)]
    reshape x14 -> x0, local copies, waits for them, and re-layouts: 36.6 us -> none  [the longest x2 10.4 us: local(): mixed_qkv.reshape(image_count, slot_count, 3, H, head_size)]
    all_to_all x8 -> x0, starting transfers between devices: 35 us -> none  [the longest x2 9.78 us: regroup_heads(): lax.all_to_all(values, 'seq', split_axis=3, concat_axis=1, tiled=True)]
  transfers between devices with their start and end apart: 17 -> 0, of which waited for: 8 -> 0; matrix products, arithmetic and copies ran while one was open for 43% -> 0% of each run, Pallas kernels for 0% -> 0%
where the time goes in v1:
time: 383 us; the launch traced here: 378 us
  Pallas kernels  362 us (95%)
  local copies, waits for them, and re-layouts  11.1 us (3%)
  other arithmetic  4.03 us (1%)
    pallas_call x6, Pallas kernels, call(): pl.pallas_call(functools.partial(kernel, dims), out_shape=[jax.ShapeDtype...  362 us

profile of v1, /device:TPU:0, one launch (start us, length us, event | category | flops | bytes accessed | tf_op | source)
XLA Modules:
  0.0 377.7 jit_solution(7623769935851977994)
XLA Ops:
  0.7 0.7 select_bitcast_fusion
  1.4 0.7 pad_add_fusion.rts
  2.1 1.4 concatenate.11
  3.5 0.1 dynamic_update_slice.3.vec
  3.7 0.0 copy-start.4
  3.7 0.6 copy-done.4
  4.3 94.5 %front.1 = (bf16[1408,512]{1,0:T(8,128)(2,1)}, bf16[4,512,512]{2,1,0:T(8,128)(2,1)}, bf16[4,512,512]{2,1,0:T(8,128)(2,1)}, bf16[512,1536]{1,0:T(8,128)(2,1)}, bf...) custom-call(bf16[12,50,512]{2,1,0:T(8,128)(2,1)} %tok.1, ...), custom_call_target="tpu_custom_call" | custom-call | tf_op jit(solution)/shard_map/front/pallas_call | solution.py:1137
  98.8 38.8 %experts.1 = (bf16[1408,512]{1,0:T(8,128)(2,1)}, bf16[4,1408,512]{2,1,0:T(8,128)(2,1)}, bf16[4,1408,512]{2,1,0:T(8,128)(2,1)}, bf16[4,3,50,512]{3,2,1,0:T(8,128)(2,1)}) custom-call(bf16[1408,512]{1,0:T(8,128)(2,1)} %get-tuple-element.44.rows, bf16[4,512,512]{2,1,0:T(8,128)(2,1)} %get-tuple-element.45.win_all, ...), custom_call_target="tpu_custom_call" | custom-call | tf_op jit(solution)/shard_map/experts/pallas_call | solution.py:1137
  137.6 27.9 %mix.1 = (bf16[1408,512]{1,0:T(8,128)(2,1)}, bf16[12,50,512]{2,1,0:T(8,128)(2,1)}, f32[3,256,512]{2,1,0:T(8,128)}, f32[3,256,128]{2,1,0:T(8,128)}, f32[8,512]{1,0:T(8,128)}) custom-call(bf16[1408,512]{1,0:T(8,128)(2,1)} %get-tuple-element.47.ret, bf16[4,3,50,512]{3,2,1,0:T(8,128)(2,1)} %get-tuple-element.48.tin, f32[3,256,512]{2,1,0:T(8,128)} %get-tuple-element.49.x2s, ...), custom_call_target="tpu_custom_call" | custom-call | tf_op jit(solution)/shard_map/mix/pallas_call | solution.py:1137
  165.6 31.7 %experts_back.1 = (bf16[1408,512]{1,0:T(8,128)(2,1)}, bf16[4,1024,512]{2,1,0:T(8,128)(2,1)}) custom-call(bf16[1408,512]{1,0:T(8,128)(2,1)} %get-tuple-element.44.rows, bf16[1408,512]{1,0:T(8,128)(2,1)} %get-tuple-element.55.drows, bf16[4,1408,512]{2,1,0:T(8,128)(2,1)} %get-tuple-element.56.acts, bf16[4,1408,512]{2,1,0:T(8,128)(2,1)} %get-tuple-element.57.slopes, ...), custom_call_target="tpu_custom_call" | custom-call | tf_op jit(solution)/shard_map/experts_back/pallas_call | solution.py:1137
  197.3 0.0 copy-start.5
  197.3 122.0 %back.1 = (bf16[12,50,512]{2,1,0:T(8,128)(2,1)}, bf16[512,2048]{1,0:T(8,128)(2,1)}, f32[8,512]{1,0:T(8,128)}, f32[512,512]{1,0:T(8,128)}, f32[512,512]{1,0:T(8,128)}) custom-call(bf16[1408,512]{1,0:T(8,128)(2,1)} %get-tuple-element.58.dret, bf16[4,1024,512]{2,1,0:T(8,128)(2,1)} %get-tuple-element.59.dws, f32[3,256,512]{2,1,0:T(8,128)} %get-tuple-element.60.dys, ...), custom_call_target="tpu_custom_call" | custom-call | tf_op jit(solution)/shard_map/back/pallas_call | solution.py:1137
  319.3 0.7 convert.6
  320.1 0.0 copy-done.5
  320.1 0.6 pad_maximum_fusion.gvec
  320.7 46.7 %dense.1 = (f32[64,2048]{1,0:T(8,128)}, f32[16,512]{1,0:T(8,128)}) custom-call(bf16[512,2048]{1,0:T(8,128)(2,1)} %get-tuple-element.70.gbig, bf16[16,512]{1,0:T(8,128)(2,1)} %pad_maximum_fusion.gvec), custom_call_target="tpu_custom_call" | custom-call | tf_op jit(solution)/shard_map/dense/pallas_call | solution.py:1137
  367.4 1.8 slice.23
  369.3 1.6 slice.24
  370.8 1.3 dynamic-slice_bitcast_fusion
  372.2 1.4 dynamic-slice_bitcast_fusion.1
  373.6 1.3 convert_element_type.4
  374.9 0.8 copy.27
  375.7 1.0 copy.28
  376.7 1.0 copy.29
  (13 shorter events, 0.0 us)
Async XLA Ops:
  3.7 0.6 copy-start.4
  197.3 122.8 %copy-start.5 = (f32[8,512]{1,0:T(8,128)S(1)}, f32[8,512]{1,0:T(8,128)}, u32[]{:S(2)}) copy-start(f32[8,512]{1,0:T(8,128)} %get-tuple-element.72) | copy-start | bytes 49156
  320.7 52.9 %copy-start.3 = (bf16[12,50,512]{2,1,0:T(8,128)(2,1)S(1)}, bf16[12,50,512]{2,1,0:T(8,128)(2,1)}, u32[]{:S(2)}) copy-start(bf16[12,50,512]{2,1,0:T(8,128)(2,1)} %get-tuple-element.69) | copy-start | bytes 1843204
  367.4 7.4 %copy-start.2 = (bf16[12,50,512]{2,1,0:T(8,128)(2,1)S(1)}, bf16[12,50,512]{2,1,0:T(8,128)(2,1)}, u32[]{:S(2)}) copy-start(bf16[12,50,512]{2,1,0:T(8,128)(2,1)} %get-tuple-element.94) | copy-start | bytes 1843204
  373.6 2.1 copy-start.1
  374.9 1.8 copy-start
